TPU v7x, 32 devices: a whole 2x2x4 slice. The times are simulated.
32 devices in a mesh: img: 4 (over z), ty: 4 (over y, core), tx: 2 (over x).
Axes of the slice: x: 2, y: 2, z: 4, core: 2. Of those that a mesh axis runs over, the one named last changes fastest.
Arguments:
- block_in: float32 [4, 64, 16, 1152], P('img', 'ty', 'tx'), may hold values from -6 to 6
- bucket: int32 [4], P('img'), may hold values from 0 to 31
- tile_anchor: int32 [4, 4, 2, 2], P('img', 'ty', 'tx'), may hold values from 0 to 255
- cond_table: float32 [32, 1152], replicated, may hold values from -6 to 6
- mod_weight: bfloat16 [1152, 6912], P(None, ('ty', 'tx')), may hold values from -0.1875 to 0.1875
- mod_bias: float32 [6912], P(('ty', 'tx')), may hold values from -3 to 3
- qkv_weight: bfloat16 [1152, 3456], replicated, may hold values from -0.1875 to 0.1875
- query_gain: float32 [72], replicated, may hold values from 0.5 to 1.5
- key_gain: float32 [72], replicated, may hold values from 0.5 to 1.5
- out_weight: bfloat16 [1152, 1152], replicated, may hold values from -3.5 to 3.5
- gate_up_weight: bfloat16 [1152, 6144], replicated, may hold values from -0.1875 to 0.1875
- down_weight: bfloat16 [3072, 1152], replicated, may hold values from -0.109375 to 0.109375
- cotangent: float32 [4, 64, 16, 1152], P('img', 'ty', 'tx'), may hold values from -6 to 6
Outputs:
- output: float32 [4, 64, 16, 1152], P('img', 'ty', 'tx')
- in_grad: float32 [4, 64, 16, 1152], P('img', 'ty', 'tx')
- table_grad: float32 [32, 1152], P(('ty', 'tx'), 'img')
- modw_grad: float32 [1152, 6912], P('img', ('ty', 'tx'))
- modb_grad: float32 [6912], P(('ty', 'tx'))
- qkv_grad: float32 [1152, 3456], P(('ty', 'tx'), 'img')
- qgain_grad: float32 [72], replicated
- kgain_grad: float32 [72], replicated
- outw_grad: float32 [1152, 1152], P(('ty', 'tx'), 'img')
- gateup_grad: float32 [1152, 6144], P(('ty', 'tx'), 'img')
- down_grad: float32 [3072, 1152], P(('ty', 'tx'), 'img')
All inputs are finite; a program needn't handle non-finite values.
Results may differ from a plain program's by a relative error of at most 0.017.
Values may be sent and summed in bfloat16 or wider, within the bound.
No kernel may reach another device: no remote copies, remote signals or barrier semaphores. Data moves between devices by JAX's collectives and lax.ppermute only.
A program may use at most 256 MiB of HBM per device.

v0:
```python
import math
import jax
import jax.numpy as jnp
from jax import lax
from jax.sharding import PartitionSpec as P

HEADS = 16
HD = 72
EPS = 1e-06
PRECISE = lax.Precision.HIGHEST


def normed(value):
    return value * lax.rsqrt(jnp.mean(value * value, axis=-1, keepdims=True) + EPS)


def norm_back(value, upstream):
    inverse = lax.rsqrt(jnp.mean(value * value, axis=-1, keepdims=True) + EPS)
    unit_value = value * inverse
    return inverse * (
        upstream - unit_value * jnp.mean(upstream * unit_value, axis=-1, keepdims=True)
    )


def rotate(value, tables, turning):
    row_cos, row_sin, col_cos, col_sin = tables
    quarter = value.shape[-1] // 4
    first = value[..., :quarter]
    second = value[..., quarter : 2 * quarter]
    third = value[..., 2 * quarter : 3 * quarter]
    fourth = value[..., 3 * quarter :]
    row_turn = turning * row_sin
    col_turn = turning * col_sin
    return jnp.concatenate(
        [
            first * row_cos - second * row_turn,
            second * row_cos + first * row_turn,
            third * col_cos - fourth * col_turn,
            fourth * col_cos + third * col_turn,
        ],
        axis=-1,
    )


def silu_slope(value):
    sigma = jax.nn.sigmoid(value)
    return sigma * (1.0 + value * (1.0 - sigma))


def product(left, right):
    return jnp.einsum("ik,kj->ij", left, right, preferred_element_type=jnp.float32)


def product_rt(left, right):
    return jnp.einsum("ik,jk->ij", left, right, preferred_element_type=jnp.float32)


def product_lt(left, right):
    return jnp.einsum("ki,kj->ij", left, right, preferred_element_type=jnp.float32)


def on_device(
    block_in,
    bucket,
    tile_anchor,
    cond_table,
    mod_weight,
    mod_bias,
    qkv_weight,
    query_gain,
    key_gain,
    out_weight,
    gate_up_weight,
    down_weight,
    cotangent,
):
    images, tile_rows, tile_cols, model_width = block_in.shape
    tokens = tile_rows * tile_cols
    all_rows = images * tokens
    head_count = HEADS
    head_size = HD
    score_scale = head_size ** (-0.5)
    hidden_units = down_weight.shape[0]
    onehot = (bucket[:, None] == jnp.arange(cond_table.shape[0], dtype=jnp.int32)[None, :]).astype(
        jnp.float32
    )
    condition = jnp.dot(onehot, cond_table, precision=PRECISE)
    cond_act = jax.nn.silu(condition).astype(jnp.bfloat16)
    mod_part = product(cond_act, mod_weight) + mod_bias[None, :]
    modulation = lax.all_gather(mod_part, ("ty", "tx"), axis=1, tiled=True)
    pieces = [
        modulation[:, None, index * model_width : (index + 1) * model_width] for index in range(6)
    ]
    shift_in, scale_in, gate_in, shift_mid, scale_mid, gate_mid = pieces
    places = jnp.arange(tokens, dtype=jnp.int32)
    row_pos = (tile_anchor[:, 0, 0, 0][:, None] + places[None, :] // tile_cols).astype(jnp.float32)
    col_pos = (tile_anchor[:, 0, 0, 1][:, None] + places[None, :] % tile_cols).astype(jnp.float32)
    quarter = head_size // 4
    frequency = jnp.exp(-math.log(10000.0) * jnp.arange(quarter, dtype=jnp.float32) / quarter)
    row_angle = row_pos[:, :, None, None] * frequency
    col_angle = col_pos[:, :, None, None] * frequency
    tables = (jnp.cos(row_angle), jnp.sin(row_angle), jnp.cos(col_angle), jnp.sin(col_angle))
    inputs = block_in.reshape(images, tokens, model_width)
    normed_in = normed(inputs)
    hidden_in = (
        (normed_in * (1.0 + scale_in) + shift_in)
        .astype(jnp.bfloat16)
        .reshape(all_rows, model_width)
    )
    qkv = product(hidden_in, qkv_weight).reshape(images, tokens, 3 * model_width)
    query_raw = qkv[..., :model_width].reshape(images, tokens, head_count, head_size)
    key_raw = qkv[..., model_width : 2 * model_width].reshape(images, tokens, head_count, head_size)
    query_unit = normed(query_raw)
    key_unit = normed(key_raw)
    query_low = rotate(query_unit * query_gain, tables, 1.0).astype(jnp.bfloat16)
    key_low = rotate(key_unit * key_gain, tables, 1.0).astype(jnp.bfloat16)
    value_low = qkv[..., 2 * model_width :].astype(jnp.bfloat16)
    keys_all, values_all = (
        lax.all_gather(
            key_low.reshape(images, tokens, model_width), ("ty", "tx"), axis=1, tiled=True
        ),
        lax.all_gather(value_low, ("ty", "tx"), axis=1, tiled=True),
    )
    key_heads = keys_all.reshape(images, -1, head_count, head_size)
    value_heads = values_all.reshape(images, -1, head_count, head_size)

    def attend(items):
        query_img, key_img, value_img = items
        scores = (
            jnp.einsum("qhd,khd->hqk", query_img, key_img, preferred_element_type=jnp.float32)
            * score_scale
        )
        row_max = jnp.max(scores, axis=-1, keepdims=True)
        expo = jnp.exp(scores - row_max)
        row_sum = jnp.sum(expo, axis=-1, keepdims=True)
        mixed = jnp.einsum(
            "hqk,khd->qhd",
            (expo / row_sum).astype(jnp.bfloat16),
            value_img,
            preferred_element_type=jnp.float32,
        )
        return (mixed, (row_max + jnp.log(row_sum))[:, :, 0])

    mixed_full, log_total = lax.map(attend, (query_low, key_heads, value_heads))
    attended = mixed_full.reshape(all_rows, model_width).astype(jnp.bfloat16)
    attn_out = product(attended, out_weight).reshape(images, tokens, model_width)
    middle = inputs + gate_in * attn_out
    normed_mid = normed(middle)
    hidden_mid = (
        (normed_mid * (1.0 + scale_mid) + shift_mid)
        .astype(jnp.bfloat16)
        .reshape(all_rows, model_width)
    )

    def feed(hidden_value):
        gate_up = product(hidden_value, gate_up_weight)
        return (gate_up[:, :hidden_units], gate_up[:, hidden_units:])

    gate_pre, up_pre = feed(hidden_mid)
    activ = (jax.nn.silu(gate_pre) * up_pre).astype(jnp.bfloat16)
    mlp_out = product(activ, down_weight).reshape(images, tokens, model_width)
    output = middle + gate_mid * mlp_out
    upstream = cotangent.reshape(images, tokens, model_width)
    gmid_grad = jnp.sum(upstream * mlp_out, axis=1)
    mlp_grad = (gate_mid * upstream).astype(jnp.bfloat16).reshape(all_rows, model_width)
    down_grad = product_lt(activ, mlp_grad)
    activ_grad = product_rt(mlp_grad, down_weight)
    gate_pre, up_pre = feed(hidden_mid)
    gu_grad = jnp.concatenate(
        [activ_grad * up_pre * silu_slope(gate_pre), activ_grad * jax.nn.silu(gate_pre)], axis=1
    ).astype(jnp.bfloat16)
    gateup_grad = product_lt(hidden_mid, gu_grad)
    mid_grad = product_rt(gu_grad, gate_up_weight).reshape(images, tokens, model_width)
    smid_grad = jnp.sum(mid_grad, axis=1)
    cmid_grad = jnp.sum(mid_grad * normed_mid, axis=1)
    middle_grad = upstream + norm_back(middle, mid_grad * (1.0 + scale_mid))
    gin_grad = jnp.sum(middle_grad * attn_out, axis=1)
    attn_grad = (gate_in * middle_grad).astype(jnp.bfloat16).reshape(all_rows, model_width)
    outw_grad = product_lt(attended, attn_grad)
    attended_grad = (
        product_rt(attn_grad, out_weight)
        .astype(jnp.bfloat16)
        .reshape(images, tokens, head_count, head_size)
    )
    row_delta = jnp.swapaxes(jnp.sum(attended_grad.astype(jnp.float32) * mixed_full, axis=-1), 1, 2)

    def score_parts(query_img, key_img, value_img, grad_img, total_img, delta_img):
        scores = (
            jnp.einsum("qhd,khd->hqk", query_img, key_img, preferred_element_type=jnp.float32)
            * score_scale
        )
        probs = jnp.exp(scores - total_img[:, :, None])
        prob_grad = jnp.einsum(
            "qhd,khd->hqk", grad_img, value_img, preferred_element_type=jnp.float32
        )
        score_grad = (probs * (prob_grad - delta_img[:, :, None])).astype(jnp.bfloat16)
        return (probs.astype(jnp.bfloat16), score_grad)

    def grads_all(items):
        query_img, key_img, value_img, grad_img, total_img, delta_img = items
        probs_low, score_grad = score_parts(
            query_img, key_img, value_img, grad_img, total_img, delta_img
        )
        query_part = (
            jnp.einsum("hqk,khd->qhd", score_grad, key_img, preferred_element_type=jnp.float32)
            * score_scale
        )
        key_part = (
            jnp.einsum("hqk,qhd->khd", score_grad, query_img, preferred_element_type=jnp.float32)
            * score_scale
        )
        value_part = jnp.einsum(
            "hqk,qhd->khd", probs_low, grad_img, preferred_element_type=jnp.float32
        )
        return (query_part, key_part.reshape(-1, model_width), value_part.reshape(-1, model_width))

    query_grad, key_full, value_full = lax.map(
        grads_all, (query_low, key_heads, value_heads, attended_grad, log_total, row_delta)
    )
    key_grad, value_grad = (
        lax.psum_scatter(
            key_full.astype(jnp.bfloat16), ("ty", "tx"), scatter_dimension=1, tiled=True
        ).astype(jnp.float32),
        lax.psum_scatter(
            value_full.astype(jnp.bfloat16), ("ty", "tx"), scatter_dimension=1, tiled=True
        ).astype(jnp.float32),
    )
    query_turned = rotate(query_grad, tables, -1.0)
    key_turned = rotate(key_grad.reshape(images, tokens, head_count, head_size), tables, -1.0)
    qgain_part = jnp.sum(query_turned * query_unit, axis=(0, 1, 2))
    kgain_part = jnp.sum(key_turned * key_unit, axis=(0, 1, 2))
    query_back = norm_back(query_raw, query_turned * query_gain).reshape(
        images, tokens, model_width
    )
    key_back = norm_back(key_raw, key_turned * key_gain).reshape(images, tokens, model_width)
    qkv_back = jnp.concatenate([query_back, key_back, value_grad], axis=-1).astype(jnp.bfloat16)
    qkv_back = qkv_back.reshape(all_rows, 3 * model_width)
    qkv_part = product_lt(hidden_in, qkv_back)
    in_back = product_rt(qkv_back, qkv_weight).reshape(images, tokens, model_width)
    sin_grad = jnp.sum(in_back, axis=1)
    cin_grad = jnp.sum(in_back * normed_in, axis=1)
    in_grad = middle_grad + norm_back(inputs, in_back * (1.0 + scale_in))
    mod_grad = jnp.concatenate(
        [sin_grad, cin_grad, gin_grad, smid_grad, cmid_grad, gmid_grad], axis=1
    )
    mod_cols = lax.psum_scatter(mod_grad, ("ty", "tx"), scatter_dimension=1, tiled=True)
    modw_part = jnp.dot(cond_act.astype(jnp.float32).T, mod_cols, precision=PRECISE)
    modb_part = jnp.sum(mod_cols, axis=0)
    act_grad = jnp.dot(mod_cols, mod_weight.astype(jnp.float32).T, precision=PRECISE)
    cond_grad = act_grad * silu_slope(condition)
    table_part = jnp.dot(onehot.T, cond_grad, precision=PRECISE)
    qkv_share, outw_share, gateup_share, down_share, table_share = (
        lax.psum_scatter(
            qkv_part.astype(jnp.bfloat16), ("ty", "tx"), scatter_dimension=0, tiled=True
        ).astype(jnp.float32),
        lax.psum_scatter(
            outw_grad.astype(jnp.bfloat16), ("ty", "tx"), scatter_dimension=0, tiled=True
        ).astype(jnp.float32),
        lax.psum_scatter(
            gateup_grad.astype(jnp.bfloat16), ("ty", "tx"), scatter_dimension=0, tiled=True
        ).astype(jnp.float32),
        lax.psum_scatter(
            down_grad.astype(jnp.bfloat16), ("ty", "tx"), scatter_dimension=0, tiled=True
        ).astype(jnp.float32),
        lax.psum_scatter(
            table_part.astype(jnp.bfloat16), ("ty", "tx"), scatter_dimension=0, tiled=True
        ).astype(jnp.float32),
    )
    qkv_total, outw_total, gateup_total, down_total, table_total = (
        lax.psum_scatter(
            qkv_share.astype(jnp.bfloat16), "img", scatter_dimension=1, tiled=True
        ).astype(jnp.float32),
        lax.psum_scatter(
            outw_share.astype(jnp.bfloat16), "img", scatter_dimension=1, tiled=True
        ).astype(jnp.float32),
        lax.psum_scatter(
            gateup_share.astype(jnp.bfloat16), "img", scatter_dimension=1, tiled=True
        ).astype(jnp.float32),
        lax.psum_scatter(
            down_share.astype(jnp.bfloat16), "img", scatter_dimension=1, tiled=True
        ).astype(jnp.float32),
        lax.psum_scatter(
            table_share.astype(jnp.bfloat16), "img", scatter_dimension=1, tiled=True
        ).astype(jnp.float32),
    )
    modw_total = lax.psum_scatter(
        modw_part.astype(jnp.bfloat16), "img", scatter_dimension=0, tiled=True
    ).astype(jnp.float32)
    modb_total = lax.psum(modb_part, "img")
    qgain_total, kgain_total = lax.psum((qgain_part, kgain_part), ("img", "ty", "tx"))
    return (
        output.reshape(block_in.shape),
        in_grad.reshape(block_in.shape),
        table_total,
        modw_total,
        modb_total,
        qkv_total,
        qgain_total,
        kgain_total,
        outw_total,
        gateup_total,
        down_total,
    )


def solution(mesh):
    return jax.shard_map(
        on_device,
        mesh=mesh,
        in_specs=(
            P("img", "ty", "tx", None),
            P("img"),
            P("img", "ty", "tx", None),
            P(),
            P(None, ("ty", "tx")),
            P(("ty", "tx")),
            P(),
            P(),
            P(),
            P(),
            P(),
            P(),
            P("img", "ty", "tx", None),
        ),
        out_specs=(
            P("img", "ty", "tx", None),
            P("img", "ty", "tx", None),
            P(("ty", "tx"), "img"),
            P("img", ("ty", "tx")),
            P(("ty", "tx")),
            P(("ty", "tx"), "img"),
            P(),
            P(),
            P(("ty", "tx"), "img"),
            P(("ty", "tx"), "img"),
            P(("ty", "tx"), "img"),
        ),
        check_vma=False,
    )
```

profile of v0, /device:TPU:0, one launch (start us, length us, event | category | flops | bytes accessed | tf_op | source)
XLA Modules:
  0.0 885.4 jit_solution(3208872247475456822)
XLA Ops:
  15.5 25.7 %all-reduce = f32[6912]{0:T(1024)S(1)} all-reduce(f32[6912]{0:T(1024)S(1)} %add_dynamic-update-slice_fusion), channel_id=2, replica_groups=mesh['img'=4,'ty'=4,'tx'=2] {'ty','tx'}, use_global_device_ids=true, to_apply=%add | all-reduce | flops 6912 | bytes 55296
  43.1 4.7 convolution_bitcast_fusion
  66.9 21.1 %all-gather.6.cloned.1.call-done = bf16[1,1024,1152]{1,2,0:T(8,128)(2,1)} async-done(((bf16[1,128,1152]{1,2,0:T(8,128)(2,1)}), bf16[1,1024,1152]{1,2,0:T(8,128)(2,1)}) %all-gather.6.cloned.1.call-update) | async-done | bytes 2359312 | tf_op jit(solution)/shard_map/all_gather | solution.py:119
  95.1 24.4 %all-gather.4.cloned.1.call-done = bf16[1,1024,1152]{2,1,0:T(8,128)(2,1)} async-done(((bf16[1,128,1152]{2,1,0:T(8,128)(2,1)}), bf16[1,1024,1152]{2,1,0:T(8,128)(2,1)}) %all-gather.4.cloned.1.call-update) | async-done | bytes 2359312 | tf_op jit(solution)/shard_map/all_gather | solution.py:122
  119.5 4.7 copy.69
  124.3 7.0 fusion.50
  132.7 4.1 fusion.45
  136.8 4.5 multiply_convert_fusion.4
  141.3 12.0 %multiply_reduce_fusion.3 = (f32[1152]{0:T(1024)}, f32[128]{0:T(128)S(1)}, f32[1152]{0:T(1024)}, f32[128,1152]{1,0:T(8,128)}) fusion(f32[128,1152]{1,0:T(8,128)S(1)} %get-tuple-element.128, f32[128]{0:T(128)S(1)} %add_rsqrt_fusion.3, f32[1152]{0:T(1024)S(1)} %get-tuple-element.113, bf16[1152,6144]{1,0:T(8,128)(2,1)} %param.23, ...), kind=kOutput, calls=%fused_computation.48 | convolution fusion | flops 1816114816 | bytes 16923136 | tf_op jit(solution)/shard_map/ik,jk->ij/dot_general | solution.py:55
  153.4 5.9 multiply_reduce_fusion.4
  164.1 5.7 multiply_convert_fusion
  171.8 8.6 copy.85
  180.4 4.1 copy.100
  184.6 5.2 fusion.7
  206.4 20.8 %reduce-scatter.40.cloned.1.call-done = bf16[128,1152]{1,0:T(8,128)(2,1)} async-done(((bf16[1024,1152]{1,0:T(8,128)(2,1)}), bf16[128,1152]{1,0:T(8,128)(2,1)}) %reduce-scatter.40.cloned.1.call-update) | async-done | bytes 294928
  237.7 35.6 %reduce-scatter.26.cloned.1.call-done = bf16[1,128,1152]{2,1,0:T(8,128)(2,1)} async-done(((bf16[1,1024,1152]{2,1,0:T(8,128)(2,1)}), bf16[1,128,1152]{2,1,0:T(8,128)(2,1)}) %reduce-scatter.26.cloned.1.call-update) | async-done | bytes 294928 | tf_op jit(solution)/shard_map/reduce_scatter | solution.py:224
  273.3 7.2 multiply_reduce_fusion.5
  283.1 48.2 %reduce-scatter.42.cloned.1.call-done = f32[864,1]{1,0:T(8,128)} async-done(((f32[6912,1]{1,0:T(8,128)}), f32[864,1]{1,0:T(8,128)}) %reduce-scatter.42.cloned.1.call-update) | async-done | bytes 3472 | tf_op jit(solution)/shard_map/reshape.98
  337.4 4.9 convolution_convert_fusion.2
  343.3 5.5 convolution_convert_fusion.1
  350.1 8.5 convolution_convert_fusion
  359.3 25.1 %all-reduce.5.cloned.1.call-done = bf16[32,1152]{1,0:T(8,128)(2,1)} async-done(((bf16[32,1152]{1,0:T(8,128)(2,1)}), bf16[32,1152]{1,0:T(8,128)(2,1)}) %all-reduce.5.cloned.1.call-update) | async-done | bytes 73744
  386.2 47.2 %reduce-scatter.32.cloned.1.call-done = bf16[144,1152]{1,0:T(8,128)(2,1)} async-done(((bf16[1152,1152]{1,0:T(8,128)(2,1)}), bf16[144,1152]{1,0:T(8,128)(2,1)}) %reduce-scatter.32.cloned.1.call-update) | async-done | bytes 331792 | tf_op jit(solution)/shard_map/reduce_scatter | solution.py:256
  437.4 65.0 %reduce-scatter.38.cloned.1.call-done = bf16[384,1152]{1,0:T(8,128)(2,1)} async-done(((bf16[3072,1152]{1,0:T(8,128)(2,1)}), bf16[384,1152]{1,0:T(8,128)(2,1)}) %reduce-scatter.38.cloned.1.call-update) | async-done | bytes 884752 | tf_op jit(solution)/shard_map/reduce_scatter | solution.py:262
  504.7 71.7 %reduce-scatter.30.cloned.1.call-done = bf16[144,3456]{1,0:T(8,128)(2,1)} async-done(((bf16[1152,3456]{1,0:T(8,128)(2,1)}), bf16[144,3456]{1,0:T(8,128)(2,1)}) %reduce-scatter.30.cloned.1.call-update) | async-done | bytes 995344 | tf_op jit(solution)/shard_map/reduce_scatter | solution.py:253
  579.1 101.5 %reduce-scatter.34.cloned.1.call-done = bf16[144,6144]{1,0:T(8,128)(2,1)} async-done(((bf16[1152,6144]{1,0:T(8,128)(2,1)}), bf16[144,6144]{1,0:T(8,128)(2,1)}) %reduce-scatter.34.cloned.1.call-update) | async-done | bytes 1769488 | tf_op jit(solution)/shard_map/reduce_scatter | solution.py:259
  680.9 39.4 %all-reduce.2 = (f32[72]{0:T(128)}, f32[72]{0:T(128)}) all-reduce(f32[72]{0:T(128)S(1)} %reduce_sum.233, f32[72]{0:T(128)S(1)} %reduce_sum.236), channel_id=1, replica_groups=mesh['img'=4,'ty'=4,'tx'=2] {'img','ty','tx'}, use_global_device_ids=true, to_apply=%region_28.29 | all-reduce | flops 144 | bytes 1152 | tf_op jit(solution)/shard_map/psum | solution.py:290
  721.3 11.1 %psum.21 = f32[864]{0:T(1024)} all-reduce(f32[864]{0:T(1024)S(1)} %bitcast_reduce_fusion), channel_id=1, replica_groups=mesh['img'=4,'ty'=4,'tx'=2] {'img'}, use_global_device_ids=true, to_apply=%region_23.24 | all-reduce | flops 864 | bytes 6912 | tf_op jit(solution)/shard_map/psum | solution.py:289
  735.9 34.5 %reduce-scatter.28.cloned.1.call-done = bf16[288,864]{1,0:T(8,128)(2,1)} async-done(((bf16[1152,864]{1,0:T(8,128)(2,1)}), bf16[288,864]{1,0:T(8,128)(2,1)}) %reduce-scatter.28.cloned.1.call-update) | async-done | bytes 497680 | tf_op jit(solution)/shard_map/reduce_scatter | solution.py:286
  772.5 24.7 %reduce-scatter.50.cloned.1.call-done = bf16[288,384]{1,0:T(8,128)(2,1)} async-done(((bf16[1152,384]{1,0:T(8,128)(2,1)}), bf16[288,384]{1,0:T(8,128)(2,1)}) %reduce-scatter.50.cloned.1.call-update) | async-done | bytes 221200
  799.2 37.7 %reduce-scatter.46.cloned.1.call-done = bf16[864,144]{1,0:T(8,128)(2,1)} async-done(((bf16[3456,144]{1,0:T(8,128)(2,1)}), bf16[864,144]{1,0:T(8,128)(2,1)}) %reduce-scatter.46.cloned.1.call-update) | async-done | bytes 248848
  838.9 37.7 %reduce-scatter.36.cloned.1.call-done = bf16[144,1536]{1,0:T(8,128)(2,1)} async-done(((bf16[144,6144]{1,0:T(8,128)(2,1)}), bf16[144,1536]{1,0:T(8,128)(2,1)}) %reduce-scatter.36.cloned.1.call-update) | async-done | bytes 442384 | tf_op jit(solution)/shard_map/reduce_scatter | solution.py:276
  (290 shorter events, 104.1 us)
Async XLA Ops:
  7.2 124.2 %copy-start = (bf16[1152,1152]{1,0:T(8,128)(2,1)S(1)}, bf16[1152,1152]{1,0:T(8,128)(2,1)}, u32[]{:S(2)}) copy-start(bf16[1152,1152]{1,0:T(8,128)(2,1)} %param.22) | copy-start | bytes 7962628
  7.2 35.9 %copy-start.4 = (f32[1,16,8,1152]{3,2,1,0:T(8,128)S(1)}, f32[1,16,8,1152]{3,2,1,0:T(8,128)}, u32[]{:S(2)}) copy-start(f32[1,16,8,1152]{3,2,1,0:T(8,128)} %param.13) | copy-start | bytes 1769476
  7.2 80.8 %all-gather.6.cloned.1.call-start = ((), (), s32[]{:S(2)}) async-start(), calls=%async_computation.14 | async-start | bytes 2654208 | tf_op jit(solution)/shard_map/all_gather | solution.py:119
  58.4 61.1 %all-gather.4.cloned.1.call-start = ((), (), s32[]{:S(2)}) async-start(), calls=%async_computation.13 | async-start | bytes 2654208 | tf_op jit(solution)/shard_map/all_gather | solution.py:122
  60.3 166.9 %reduce-scatter.40.cloned.1.call-start = ((), (), s32[]{:S(2)}) async-start(), calls=%async_computation.22 | async-start | bytes 2654208
  66.9 24.2 %copy-start.22 = (bf16[128,16,18]{0,2,1:T(8,128)(2,1)}, bf16[128,16,18]{0,2,1:T(8,128)(2,1)S(1)}, u32[]{:S(2)}) copy-start(bf16[128,16,18]{0,2,1:T(8,128)(2,1)S(1)} %get-tuple-element.144) | copy-start | bytes 221188
  66.9 24.2 %copy-start.24 = (bf16[128,16,18]{0,2,1:T(8,128)(2,1)}, bf16[128,16,18]{0,2,1:T(8,128)(2,1)S(1)}, u32[]{:S(2)}) copy-start(bf16[128,16,18]{0,2,1:T(8,128)(2,1)S(1)} %get-tuple-element.145) | copy-start | bytes 221188
  66.9 24.2 %copy-start.26 = (bf16[128,16,18]{0,2,1:T(8,128)(2,1)}, bf16[128,16,18]{0,2,1:T(8,128)(2,1)S(1)}, u32[]{:S(2)}) copy-start(bf16[128,16,18]{0,2,1:T(8,128)(2,1)S(1)} %get-tuple-element.158) | copy-start | bytes 221188
  94.5 29.7 %copy-start.61 = (f32[16,128]{1,0:T(8,128)}, f32[16,128]{1,0:T(8,128)S(1)}, u32[]{:S(2)}) copy-start(f32[16,128]{1,0:T(8,128)S(1)} %fusion) | copy-start | bytes 24580
  184.5 88.7 %reduce-scatter.26.cloned.1.call-start = ((), (), s32[]{:S(2)}) async-start(), calls=%async_computation.15 | async-start | bytes 2654208 | tf_op jit(solution)/shard_map/reduce_scatter | solution.py:224
  192.4 138.9 %reduce-scatter.42.cloned.1.call-start = ((), (), s32[]{:S(2)}) async-start(), calls=%async_computation.23 | async-start | bytes 3981312 | tf_op jit(solution)/shard_map/reshape.98
  205.3 25.0 %copy-start.12 = (f32[1,128,1152]{1,2,0:T(8,128)S(1)}, f32[1,128,1152]{1,2,0:T(8,128)}, u32[]{:S(2)}) copy-start(f32[1,128,1152]{1,2,0:T(8,128)} %copy.71) | copy-start | bytes 1769476
  234.2 39.1 %copy-start.65 = (f32[128]{0:T(128)S(1)}, f32[128]{0:T(128)}, u32[]{:S(2)}) copy-start(f32[128]{0:T(128)} %copy-done.64) | copy-start | bytes 1540
  283.0 50.9 %copy-start.50 = (f32[1152]{0:T(1024)S(1)}, f32[1152]{0:T(1024)}, u32[]{:S(2)}) copy-start(f32[1152]{0:T(1024)} %copy-done.49) | copy-start | bytes 13828
  283.0 52.0 %copy-start.10 = (f32[128,1152]{1,0:T(8,128)S(1)}, f32[128,1152]{1,0:T(8,128)}, u32[]{:S(2)}) copy-start(f32[128,1152]{1,0:T(8,128)} %copy-done.9) | copy-start | bytes 1769476
  283.0 52.0 %copy-start.40 = (f32[1152]{0:T(1024)S(1)}, f32[1152]{0:T(1024)}, u32[]{:S(2)}) copy-start(f32[1152]{0:T(1024)} %get-tuple-element.116) | copy-start | bytes 13828
  283.0 101.4 %all-reduce.5.cloned.1.call-start = ((), (), s32[]{:S(2)}) async-start(), calls=%async_computation.28 | async-start | bytes 147456
  334.7 98.7 %reduce-scatter.32.cloned.1.call-start = ((), (), s32[]{:S(2)}) async-start(), calls=%async_computation.18 | async-start | bytes 2985984 | tf_op jit(solution)/shard_map/reduce_scatter | solution.py:256
  337.4 165.1 %reduce-scatter.38.cloned.1.call-start = ((), (), s32[]{:S(2)}) async-start(), calls=%async_computation.21 | async-start | bytes 7962624 | tf_op jit(solution)/shard_map/reduce_scatter | solution.py:262
  342.4 234.0 %reduce-scatter.30.cloned.1.call-start = ((), (), s32[]{:S(2)}) async-start(), calls=%async_computation.17 | async-start | bytes 8957952 | tf_op jit(solution)/shard_map/reduce_scatter | solution.py:253
  348.8 331.8 %reduce-scatter.34.cloned.1.call-start = ((), (), s32[]{:S(2)}) async-start(), calls=%async_computation.19 | async-start | bytes 15925248 | tf_op jit(solution)/shard_map/reduce_scatter | solution.py:259
  358.6 76.9 %copy-start.21 = (f32[864,1]{1,0:T(8,128)S(1)}, f32[864,1]{1,0:T(8,128)}, u32[]{:S(2)}) copy-start(f32[864,1]{1,0:T(8,128)} %reduce-scatter.42.cloned.1.call-done) | copy-start | bytes 10372
  358.6 77.1 %copy-start.54 = (f32[1152]{0:T(1024)S(1)}, f32[1152]{0:T(1024)}, u32[]{:S(2)}) copy-start(f32[1152]{0:T(1024)} %get-tuple-element.119) | copy-start | bytes 13828
  358.6 373.8 %reduce-scatter.44.cloned.1.call-start = ((), (), s32[]{:S(2)}) async-start(), calls=%async_computation.24 | async-start | bytes 368640
  386.1 348.0 %reduce-scatter.48.cloned.1.call-start = ((), (), s32[]{:S(2)}) async-start(), calls=%async_computation.26 | async-start | bytes 737280
  435.4 335.0 %reduce-scatter.28.cloned.1.call-start = ((), (), s32[]{:S(2)}) async-start(), calls=%async_computation.16 | async-start | bytes 2580480 | tf_op jit(solution)/shard_map/reduce_scatter | solution.py:286
  437.4 359.8 %reduce-scatter.50.cloned.1.call-start = ((), (), s32[]{:S(2)}) async-start(), calls=%async_computation.27 | async-start | bytes 1105920
  504.7 215.6 %copy-start.70 = (f32[128]{0:T(128)S(1)}, f32[128]{0:T(128)}, u32[]{:S(2)}) copy-start(f32[128]{0:T(128)} %get-tuple-element.108) | copy-start | bytes 1540
  504.7 215.6 %copy-start.29 = (f32[128,1152]{1,0:T(8,128)S(1)}, f32[128,1152]{1,0:T(8,128)}, u32[]{:S(2)}) copy-start(f32[128,1152]{1,0:T(8,128)} %get-tuple-element.181) | copy-start | bytes 1769476
  504.7 332.2 %reduce-scatter.46.cloned.1.call-start = ((), (), s32[]{:S(2)}) async-start(), calls=%async_computation.25 | async-start | bytes 2211840
  579.0 297.6 %reduce-scatter.36.cloned.1.call-start = ((), (), s32[]{:S(2)}) async-start(), calls=%async_computation.20 | async-start | bytes 2211840 | tf_op jit(solution)/shard_map/reduce_scatter | solution.py:276
  732.4 146.2 %copy-start.1 = (bf16[1152,1152]{1,0:T(8,128)(2,1)S(1)}, bf16[1152,1152]{1,0:T(8,128)(2,1)}, u32[]{:S(2)}) copy-start(bf16[1152,1152]{1,0:T(8,128)(2,1)} %param.22) | copy-start | bytes 7962628
  (61 other events, 308.1 us)
Sparse Core Ops, SparseCore 0:
  58.5 29.4 all-gather.5
  90.5 28.9 all-gather.3
  184.7 42.4 reduce-scatter.39
  230.8 42.4 reduce-scatter.25
  283.1 48.0 reduce-scatter.41
  334.8 49.5 all-reduce.4
  388.4 44.9 reduce-scatter.31
  436.9 65.5 reduce-scatter.37
  506.4 70.0 reduce-scatter.29
  579.9 100.7 reduce-scatter.33
  683.5 20.0 reduce-scatter.43
  706.3 20.2 reduce-scatter.47
  728.9 41.4 reduce-scatter.27
  773.2 23.8 reduce-scatter.49
  799.5 37.3 reduce-scatter.45
  839.1 37.4 reduce-scatter.35
where the time goes:
time: 892 us; the launch traced here: 885 us
  waiting for transfers between devices  595 us (67%)
  matrix products  93.7 us (11%)
  blocking collectives  76.2 us (9%)
  local copies, waits for them, and re-layouts  70.6 us (8%)
  other arithmetic  31.3 us (4%)
  between operations  17.3 us (2%)
    unnamed x22, waiting for transfers between devices  109 us
    reduce_scatter x1, waiting for transfers between devices, on_device(): lax.psum_scatter(gateup_grad.astype(jnp.bfloat16), ('ty', 'tx'), scatter_...  102 us
    reduce_scatter x1, waiting for transfers between devices, on_device(): lax.psum_scatter(qkv_part.astype(jnp.bfloat16), ('ty', 'tx'), scatter_dim...  71.7 us
    reduce_scatter x1, waiting for transfers between devices, on_device(): lax.psum_scatter(down_grad.astype(jnp.bfloat16), ('ty', 'tx'), scatter_di...  65 us
    another operation x1, waiting for transfers between devices  48.2 us
    reduce_scatter x1, waiting for transfers between devices, on_device(): lax.psum_scatter(outw_grad.astype(jnp.bfloat16), ('ty', 'tx'), scatter_di...  47.2 us
    unnamed x176, local copies, waits for them, and re-layouts  40.9 us
    psum x1, blocking collectives, on_device(): lax.psum((qgain_part, kgain_part), ('img', 'ty', 'tx'))  39.4 us
  transfers between devices with their start and end apart: 16, of which 14 were waited for; matrix products, arithmetic and copies ran while one was open for 10% of the time, Pallas kernels for 0%

commit v1 on v0

--- a/solution.py
+++ b/solution.py
@@ -1,3 +1,4 @@
+import functools
 import math
 import jax
 import jax.numpy as jnp
@@ -8,6 +9,23 @@
 HD = 72
 EPS = 1e-06
 PRECISE = lax.Precision.HIGHEST
+
+
+def see_the_leaf(state, ax_name, axis_no):
+    f_next, fresh = (lax.axis_size(ax_name), lax.axis_index(ax_name))
+    o_now, y1 = (state, 1)
+    while y1 < f_next:
+        current_block = lax.ppermute(
+            o_now, axis_name=ax_name, perm=[(dd, dd ^ y1) for dd in range(f_next)]
+        )
+        res = jnp.concatenate([o_now, current_block], axis=axis_no)
+        z_new = jnp.concatenate([current_block, o_now], axis=axis_no)
+        o_now = jnp.where(fresh & y1 == 0, res, z_new)
+        y1 = 2 * y1
+    return o_now
+
+
+put_tokens = functools.partial(see_the_leaf, ax_name=("ty", "tx"), axis_no=1)
 
 
 def normed(value):
@@ -119,7 +137,7 @@
         lax.all_gather(
             key_low.reshape(images, tokens, model_width), ("ty", "tx"), axis=1, tiled=True
         ),
-        lax.all_gather(value_low, ("ty", "tx"), axis=1, tiled=True),
+        put_tokens(value_low),
     )
     key_heads = keys_all.reshape(images, -1, head_count, head_size)
     value_heads = values_all.reshape(images, -1, head_count, head_size)

time: 892 us -> 887 us (level)
  waiting for transfers between devices: 595 us -> 576 us
    ppermute x0 -> x3, waiting for transfers between devices: none -> 26.1 us  [see_the_leaf(): lax.ppermute(o_now, axis_name=ax_name, perm=[(dd, dd ^ y1) for dd in rang...]
    all_gather x1 -> x0, waiting for transfers between devices: 24.4 us -> none  [on_device(): lax.all_gather(value_low, ('ty', 'tx'), axis=1, tiled=True)]
    all_gather x1, waiting for transfers between devices: 21.1 us -> 0.01 us  [on_device(): lax.all_gather(key_low.reshape(images, tokens, model_width), ('ty', 'tx')...]
    unnamed x22 -> x21, waiting for transfers between devices: 109 us -> 108 us
    unnamed x176 -> x180, local copies, waits for them, and re-layouts: 40.9 us -> 41.4 us
  transfers between devices with their start and end apart: 16 -> 18, of which waited for: 14 -> 14; matrix products, arithmetic and copies ran while one was open for 10% -> 11% of each run, Pallas kernels for 0% -> 0%
where the time goes in v1:
time: 887 us; the launch traced here: 879 us
  waiting for transfers between devices  576 us (65%)
  matrix products  93.9 us (11%)
  blocking collectives  76.2 us (9%)
  local copies, waits for them, and re-layouts  73.9 us (8%)
  other arithmetic  38.7 us (4%)
  between operations  17.4 us (2%)
    unnamed x21, waiting for transfers between devices  108 us
    reduce_scatter x1, waiting for transfers between devices, on_device(): lax.psum_scatter(gateup_grad.astype(jnp.bfloat16), ('ty', 'tx'), scatter_...  102 us
    reduce_scatter x1, waiting for transfers between devices, on_device(): lax.psum_scatter(qkv_part.astype(jnp.bfloat16), ('ty', 'tx'), scatter_dim...  71.7 us
    reduce_scatter x1, waiting for transfers between devices, on_device(): lax.psum_scatter(down_grad.astype(jnp.bfloat16), ('ty', 'tx'), scatter_di...  65 us
    another operation x1, waiting for transfers between devices  48.2 us
    reduce_scatter x1, waiting for transfers between devices, on_device(): lax.psum_scatter(outw_grad.astype(jnp.bfloat16), ('ty', 'tx'), scatter_di...  47.1 us
    unnamed x180, local copies, waits for them, and re-layouts  41.4 us
    psum x1, blocking collectives, on_device(): lax.psum((qgain_part, kgain_part), ('img', 'ty', 'tx'))  39.5 us
  transfers between devices with their start and end apart: 18, of which 14 were waited for; matrix products, arithmetic and copies ran while one was open for 11% of the time, Pallas kernels for 0%

profile of v1, /device:TPU:0, one launch (start us, length us, event | category | flops | bytes accessed | tf_op | source)
XLA Modules:
  0.0 878.6 jit_solution(1776709323222877899)
XLA Ops:
  15.5 25.7 %all-reduce = f32[6912]{0:T(1024)S(1)} all-reduce(f32[6912]{0:T(1024)S(1)} %add_dynamic-update-slice_fusion), channel_id=2, replica_groups=mesh['img'=4,'ty'=4,'tx'=2] {'ty','tx'}, use_global_device_ids=true, to_apply=%add | all-reduce | flops 6912 | bytes 55296
  42.1 4.7 convolution_bitcast_fusion
  58.6 9.0 %collective-permute-done = bf16[1,128,1152]{2,1,0:T(8,128)(2,1)} collective-permute-done((bf16[1,128,1152]{2,1,0:T(8,128)(2,1)S(1)}, bf16[1,128,1152]{2,1,0:T(8,128)(2,1)}, u32[]{:S(2)}, u32[]{:S(2)}) %collective-permute-start) | collective-permute-done | bytes 294944 | tf_op jit(solution)/shard_map/ppermute | solution.py:18
  91.4 17.1 %collective-permute-done.2 = bf16[1,512,1152]{2,1,0:T(8,128)(2,1)} collective-permute-done((bf16[1,512,1152]{2,1,0:T(8,128)(2,1)}, bf16[1,512,1152]{2,1,0:T(8,128)(2,1)}, u32[]{:S(2)}, u32[]{:S(2)}) %collective-permute-start.2) | collective-permute-done | bytes 1179680 | tf_op jit(solution)/shard_map/ppermute | solution.py:18
  110.9 3.1 multiply_reduce_fusion
  117.7 4.3 fusion.53
  122.9 8.0 fusion.48
  133.4 12.0 %multiply_reduce_fusion.3 = (f32[1152]{0:T(1024)}, f32[128]{0:T(128)S(1)}, f32[1152]{0:T(1024)}, f32[128,1152]{1,0:T(8,128)}) fusion(f32[128,1152]{1,0:T(8,128)S(1)} %get-tuple-element.128, f32[128]{0:T(128)S(1)} %add_rsqrt_fusion.3, f32[1152]{0:T(1024)S(1)} %get-tuple-element.113, bf16[1152,6144]{1,0:T(8,128)(2,1)} %param.23, ...), kind=kOutput, calls=%fused_computation.55 | convolution fusion | flops 1816114816 | bytes 16923136 | tf_op jit(solution)/shard_map/ik,jk->ij/dot_general | solution.py:73
  145.5 5.9 multiply_reduce_fusion.4
  156.2 6.7 multiply_convert_fusion
  164.9 8.6 copy.100
  173.5 4.1 copy.115
  177.7 5.2 fusion.7
  193.6 3.8 fusion.11
  200.0 20.2 %reduce-scatter.40.cloned.1.call-done = bf16[128,1152]{1,0:T(8,128)(2,1)} async-done(((bf16[1024,1152]{1,0:T(8,128)(2,1)}), bf16[128,1152]{1,0:T(8,128)(2,1)}) %reduce-scatter.40.cloned.1.call-update) | async-done | bytes 294928
  230.0 36.5 %reduce-scatter.26.cloned.1.call-done = bf16[1,128,1152]{2,1,0:T(8,128)(2,1)} async-done(((bf16[1,1024,1152]{2,1,0:T(8,128)(2,1)}), bf16[1,128,1152]{2,1,0:T(8,128)(2,1)}) %reduce-scatter.26.cloned.1.call-update) | async-done | bytes 294928 | tf_op jit(solution)/shard_map/reduce_scatter | solution.py:242
  266.5 7.2 multiply_reduce_fusion.5
  276.3 48.2 %reduce-scatter.42.cloned.1.call-done = f32[864,1]{1,0:T(8,128)} async-done(((f32[6912,1]{1,0:T(8,128)}), f32[864,1]{1,0:T(8,128)}) %reduce-scatter.42.cloned.1.call-update) | async-done | bytes 3472 | tf_op jit(solution)/shard_map/reshape.98
  330.7 4.9 convolution_convert_fusion.2
  336.6 5.5 convolution_convert_fusion.1
  343.3 8.5 convolution_convert_fusion
  352.6 25.1 %all-reduce.5.cloned.1.call-done = bf16[32,1152]{1,0:T(8,128)(2,1)} async-done(((bf16[32,1152]{1,0:T(8,128)(2,1)}), bf16[32,1152]{1,0:T(8,128)(2,1)}) %all-reduce.5.cloned.1.call-update) | async-done | bytes 73744
  379.4 47.1 %reduce-scatter.32.cloned.1.call-done = bf16[144,1152]{1,0:T(8,128)(2,1)} async-done(((bf16[1152,1152]{1,0:T(8,128)(2,1)}), bf16[144,1152]{1,0:T(8,128)(2,1)}) %reduce-scatter.32.cloned.1.call-update) | async-done | bytes 331792 | tf_op jit(solution)/shard_map/reduce_scatter | solution.py:274
  430.5 65.0 %reduce-scatter.38.cloned.1.call-done = bf16[384,1152]{1,0:T(8,128)(2,1)} async-done(((bf16[3072,1152]{1,0:T(8,128)(2,1)}), bf16[384,1152]{1,0:T(8,128)(2,1)}) %reduce-scatter.38.cloned.1.call-update) | async-done | bytes 884752 | tf_op jit(solution)/shard_map/reduce_scatter | solution.py:280
  497.8 71.7 %reduce-scatter.30.cloned.1.call-done = bf16[144,3456]{1,0:T(8,128)(2,1)} async-done(((bf16[1152,3456]{1,0:T(8,128)(2,1)}), bf16[144,3456]{1,0:T(8,128)(2,1)}) %reduce-scatter.30.cloned.1.call-update) | async-done | bytes 995344 | tf_op jit(solution)/shard_map/reduce_scatter | solution.py:271
  572.1 101.7 %reduce-scatter.34.cloned.1.call-done = bf16[144,6144]{1,0:T(8,128)(2,1)} async-done(((bf16[1152,6144]{1,0:T(8,128)(2,1)}), bf16[144,6144]{1,0:T(8,128)(2,1)}) %reduce-scatter.34.cloned.1.call-update) | async-done | bytes 1769488 | tf_op jit(solution)/shard_map/reduce_scatter | solution.py:277
  674.1 39.5 %all-reduce.2 = (f32[72]{0:T(128)}, f32[72]{0:T(128)}) all-reduce(f32[72]{0:T(128)S(1)} %reduce_sum.233, f32[72]{0:T(128)S(1)} %reduce_sum.236), channel_id=1, replica_groups=mesh['img'=4,'ty'=4,'tx'=2] {'img','ty','tx'}, use_global_device_ids=true, to_apply=%region_28.29 | all-reduce | flops 144 | bytes 1152 | tf_op jit(solution)/shard_map/psum | solution.py:308
  714.6 11.0 %psum.21 = f32[864]{0:T(1024)} all-reduce(f32[864]{0:T(1024)S(1)} %bitcast_reduce_fusion), channel_id=1, replica_groups=mesh['img'=4,'ty'=4,'tx'=2] {'img'}, use_global_device_ids=true, to_apply=%region_23.24 | all-reduce | flops 864 | bytes 6912 | tf_op jit(solution)/shard_map/psum | solution.py:307
  729.0 34.4 %reduce-scatter.28.cloned.1.call-done = bf16[288,864]{1,0:T(8,128)(2,1)} async-done(((bf16[1152,864]{1,0:T(8,128)(2,1)}), bf16[288,864]{1,0:T(8,128)(2,1)}) %reduce-scatter.28.cloned.1.call-update) | async-done | bytes 497680 | tf_op jit(solution)/shard_map/reduce_scatter | solution.py:304
  765.6 24.7 %reduce-scatter.50.cloned.1.call-done = bf16[288,384]{1,0:T(8,128)(2,1)} async-done(((bf16[1152,384]{1,0:T(8,128)(2,1)}), bf16[288,384]{1,0:T(8,128)(2,1)}) %reduce-scatter.50.cloned.1.call-update) | async-done | bytes 221200
  792.4 37.7 %reduce-scatter.46.cloned.1.call-done = bf16[864,144]{1,0:T(8,128)(2,1)} async-done(((bf16[3456,144]{1,0:T(8,128)(2,1)}), bf16[864,144]{1,0:T(8,128)(2,1)}) %reduce-scatter.46.cloned.1.call-update) | async-done | bytes 248848
  832.1 37.7 %reduce-scatter.36.cloned.1.call-done = bf16[144,1536]{1,0:T(8,128)(2,1)} async-done(((bf16[144,6144]{1,0:T(8,128)(2,1)}), bf16[144,1536]{1,0:T(8,128)(2,1)}) %reduce-scatter.36.cloned.1.call-update) | async-done | bytes 442384 | tf_op jit(solution)/shard_map/reduce_scatter | solution.py:294
  (305 shorter events, 116.3 us)
Async XLA Ops:
  7.2 114.9 %copy-start = (bf16[1152,1152]{1,0:T(8,128)(2,1)S(1)}, bf16[1152,1152]{1,0:T(8,128)(2,1)}, u32[]{:S(2)}) copy-start(bf16[1152,1152]{1,0:T(8,128)(2,1)} %param.22) | copy-start | bytes 7962628
  7.2 34.6 %copy-start.3 = (f32[1,16,8,1152]{3,2,1,0:T(8,128)S(1)}, f32[1,16,8,1152]{3,2,1,0:T(8,128)}, u32[]{:S(2)}) copy-start(f32[1,16,8,1152]{3,2,1,0:T(8,128)} %param.13) | copy-start | bytes 1769476
  7.2 103.7 %all-gather.3.cloned.1.call-start = ((), (), s32[]{:S(2)}) async-start(), calls=%async_computation.13 | async-start | bytes 2654208 | tf_op jit(solution)/shard_map/all_gather | solution.py:137
  57.3 162.9 %reduce-scatter.40.cloned.1.call-start = ((), (), s32[]{:S(2)}) async-start(), calls=%async_computation.21 | async-start | bytes 2654208
  58.5 9.1 %collective-permute-start = (bf16[1,128,1152]{2,1,0:T(8,128)(2,1)S(1)}, bf16[1,128,1152]{2,1,0:T(8,128)(2,1)}, u32[]{:S(2)}, u32[]{:S(2)}) collective-permute-start(bf16[1,128,1152]{2,1,0:T(8,128)(2,1)S(1)} %slice.220), channel_id=1, source_target_pairs={{0,1},{1,0},{2,3},{3,2},{4,5},{5,4},{6,7},{7,6},{8,9},{9,8},{10,11... | collective-permute-start | bytes 884744 | tf_op jit(solution)/shard_map/ppermute | solution.py:18
  68.8 2.4 collective-permute-start.1
  73.5 35.0 %collective-permute-start.2 = (bf16[1,512,1152]{2,1,0:T(8,128)(2,1)}, bf16[1,512,1152]{2,1,0:T(8,128)(2,1)}, u32[]{:S(2)}, u32[]{:S(2)}) collective-permute-start(bf16[1,512,1152]{2,1,0:T(8,128)(2,1)} %maximum_select_fusion.2), channel_id=1, source_target_pairs={{0,4},{1,5},{2,6},{3,7},{4,0},{5,1},{6,2},{7,3},{8,12},{9,13},{10,... | collective-permute-start | bytes 3538952 | tf_op jit(solution)/shard_map/ppermute | solution.py:18
  177.6 88.8 %reduce-scatter.26.cloned.1.call-start = ((), (), s32[]{:S(2)}) async-start(), calls=%async_computation.14 | async-start | bytes 2654208 | tf_op jit(solution)/shard_map/reduce_scatter | solution.py:242
  185.5 139.0 %reduce-scatter.42.cloned.1.call-start = ((), (), s32[]{:S(2)}) async-start(), calls=%async_computation.22 | async-start | bytes 3981312 | tf_op jit(solution)/shard_map/reshape.98
  198.9 23.4 %copy-start.39 = (f32[128,18]{0,1:T(8,128)S(1)}, f32[128,18]{0,1:T(8,128)}, u32[]{:S(2)}) copy-start(f32[128,18]{0,1:T(8,128)} %copy-done.37) | copy-start | bytes 27652
  198.9 23.4 %copy-start.52 = (f32[128,18]{0,1:T(8,128)S(1)}, f32[128,18]{0,1:T(8,128)}, u32[]{:S(2)}) copy-start(f32[128,18]{0,1:T(8,128)} %get-tuple-element.162) | copy-start | bytes 27652
  198.9 23.4 %copy-start.54 = (f32[128,18]{0,1:T(8,128)S(1)}, f32[128,18]{0,1:T(8,128)}, u32[]{:S(2)}) copy-start(f32[128,18]{0,1:T(8,128)} %get-tuple-element.172) | copy-start | bytes 27652
  227.6 38.9 %copy-start.71 = (f32[128]{0:T(128)S(1)}, f32[128]{0:T(128)}, u32[]{:S(2)}) copy-start(f32[128]{0:T(128)} %copy-done.70) | copy-start | bytes 1540
  276.2 50.9 %copy-start.58 = (f32[1152]{0:T(1024)S(1)}, f32[1152]{0:T(1024)}, u32[]{:S(2)}) copy-start(f32[1152]{0:T(1024)} %copy-done.57) | copy-start | bytes 13828
  276.2 51.8 %copy-start.10 = (f32[128,1152]{1,0:T(8,128)S(1)}, f32[128,1152]{1,0:T(8,128)}, u32[]{:S(2)}) copy-start(f32[128,1152]{1,0:T(8,128)} %copy-done.9) | copy-start | bytes 1769476
  276.2 51.8 %copy-start.46 = (f32[1152]{0:T(1024)S(1)}, f32[1152]{0:T(1024)}, u32[]{:S(2)}) copy-start(f32[1152]{0:T(1024)} %get-tuple-element.116) | copy-start | bytes 13828
  276.2 101.4 %all-reduce.5.cloned.1.call-start = ((), (), s32[]{:S(2)}) async-start(), calls=%async_computation.27 | async-start | bytes 147456
  327.9 98.5 %reduce-scatter.32.cloned.1.call-start = ((), (), s32[]{:S(2)}) async-start(), calls=%async_computation.17 | async-start | bytes 2985984 | tf_op jit(solution)/shard_map/reduce_scatter | solution.py:274
  330.4 165.1 %reduce-scatter.38.cloned.1.call-start = ((), (), s32[]{:S(2)}) async-start(), calls=%async_computation.20 | async-start | bytes 7962624 | tf_op jit(solution)/shard_map/reduce_scatter | solution.py:280
  335.6 233.9 %reduce-scatter.30.cloned.1.call-start = ((), (), s32[]{:S(2)}) async-start(), calls=%async_computation.16 | async-start | bytes 8957952 | tf_op jit(solution)/shard_map/reduce_scatter | solution.py:271
  342.0 331.8 %reduce-scatter.34.cloned.1.call-start = ((), (), s32[]{:S(2)}) async-start(), calls=%async_computation.18 | async-start | bytes 15925248 | tf_op jit(solution)/shard_map/reduce_scatter | solution.py:277
  351.8 76.7 %copy-start.22 = (f32[864,1]{1,0:T(8,128)S(1)}, f32[864,1]{1,0:T(8,128)}, u32[]{:S(2)}) copy-start(f32[864,1]{1,0:T(8,128)} %reduce-scatter.42.cloned.1.call-done) | copy-start | bytes 10372
  351.8 76.9 %copy-start.61 = (f32[1152]{0:T(1024)S(1)}, f32[1152]{0:T(1024)}, u32[]{:S(2)}) copy-start(f32[1152]{0:T(1024)} %get-tuple-element.119) | copy-start | bytes 13828
  351.9 373.8 %reduce-scatter.44.cloned.1.call-start = ((), (), s32[]{:S(2)}) async-start(), calls=%async_computation.23 | async-start | bytes 368640
  379.3 348.0 %reduce-scatter.48.cloned.1.call-start = ((), (), s32[]{:S(2)}) async-start(), calls=%async_computation.25 | async-start | bytes 737280
  428.5 334.9 %reduce-scatter.28.cloned.1.call-start = ((), (), s32[]{:S(2)}) async-start(), calls=%async_computation.15 | async-start | bytes 2580480 | tf_op jit(solution)/shard_map/reduce_scatter | solution.py:304
  430.5 359.9 %reduce-scatter.50.cloned.1.call-start = ((), (), s32[]{:S(2)}) async-start(), calls=%async_computation.26 | async-start | bytes 1105920
  497.7 332.4 %reduce-scatter.46.cloned.1.call-start = ((), (), s32[]{:S(2)}) async-start(), calls=%async_computation.24 | async-start | bytes 2211840
  572.1 141.6 %copy-start.76 = (f32[128]{0:T(128)S(1)}, f32[128]{0:T(128)}, u32[]{:S(2)}) copy-start(f32[128]{0:T(128)} %get-tuple-element.108) | copy-start | bytes 1540
  572.1 141.6 %copy-start.33 = (f32[128,1152]{1,0:T(8,128)S(1)}, f32[128,1152]{1,0:T(8,128)}, u32[]{:S(2)}) copy-start(f32[128,1152]{1,0:T(8,128)} %get-tuple-element.181) | copy-start | bytes 1769476
  572.1 297.7 %reduce-scatter.36.cloned.1.call-start = ((), (), s32[]{:S(2)}) async-start(), calls=%async_computation.19 | async-start | bytes 2211840 | tf_op jit(solution)/shard_map/reduce_scatter | solution.py:294
  763.4 108.4 %copy-start.1 = (bf16[1152,1152]{1,0:T(8,128)(2,1)S(1)}, bf16[1152,1152]{1,0:T(8,128)(2,1)}, u32[]{:S(2)}) copy-start(bf16[1152,1152]{1,0:T(8,128)(2,1)} %param.22) | copy-start | bytes 7962628
  (65 other events, 418.1 us)
Sparse Core Ops, SparseCore 0:
  57.4 35.8 all-gather.2
  177.8 42.4 reduce-scatter.39
  224.0 42.4 reduce-scatter.25
  276.4 48.0 reduce-scatter.41
  328.0 49.5 all-reduce.4
  381.4 44.9 reduce-scatter.31
  430.0 65.4 reduce-scatter.37
  499.4 70.0 reduce-scatter.29
  573.1 100.7 reduce-scatter.33
  676.5 20.0 reduce-scatter.43
  699.5 20.1 reduce-scatter.47
  721.9 41.4 reduce-scatter.27
  766.4 23.8 reduce-scatter.49
  792.6 37.3 reduce-scatter.45
  832.2 37.5 reduce-scatter.35
